TPU v7x, 32 devices: a whole 2x2x4 slice. The times are simulated.
32 devices in a mesh: groups: 2 (over y), date: 4 (over x, core), col: 4 (over z).
Axes of the slice: x: 2, y: 2, z: 4, core: 2. Of those that a mesh axis runs over, the one named last changes fastest.
Arguments:
- scenes: bfloat16 [16, 2, 128, 1024], P('date', None, 'groups', 'col'), parts along dimension 2, may hold values from -6 to 6
- pair_dates: int32 [96, 2], P('date'), may hold values from 0 to 15, as said below
- pair_count: int32 [4], P('date'), may hold values from 12 to 24, as said below
- inverse: float32 [15, 96], replicated, may hold values from -0.625 to 0.625
Outputs:
- series: float32 [15, 2, 64, 128], P(None, None, ('groups', 'date'), 'col'), parts along dimension 2
There are 2 independent parts, one for each index of `groups`. A program takes and returns all parts, laid end to end along the dimension named above; an argument that names none is the same for every part. Nothing has to cross between parts.
Inputs may be any that keep to these rules, and one draw needn't show every extreme that they name: `pair_dates`: each row names a reference acquisition and a later secondary one. Slots i * 24 to (i + 1) * 24 - 1 belong to owner i (index i of date); every slot of owner i names acquisitions held by indices i - 2 to i + 2 of date (as far as these exist), and one live pair of every owner names the lowest and the highest acquisition of that range. `pair_count`: entry i is the number of live slots of owner i; they come first in its block and the other slots are ignored. Some owner has all its slots live.
All inputs are finite; a program needn't handle non-finite values.
Results may differ from a plain program's by a relative error of at most 0.0003.
Values may be sent and summed in bfloat16 or wider, within the bound.
A program may use at most 64 MiB of HBM per device.

v0:
```python
import jax
import jax.numpy as jnp
from jax import lax
from jax.sharding import PartitionSpec as P


def padded(cells, sides, width):
    for axis, dim in sides:
        count = lax.axis_size(axis)
        ends = count - 1
        head = lax.slice_in_dim(cells, 0, width, axis=dim)
        tail = lax.slice_in_dim(cells, cells.shape[dim] - width, cells.shape[dim], axis=dim)
        cells = jnp.concatenate(
            [
                lax.ppermute(tail, axis, [(i, (i + 1) % count) for i in range(ends)]),
                cells,
                lax.ppermute(head, axis, [((i + 1) % count, i) for i in range(ends)]),
            ],
            axis=dim,
        )
    return cells


def look_matrix(padded_width, looks_here):
    column = jnp.arange(padded_width, dtype=jnp.int32)[:, None]
    target = jnp.arange(looks_here, dtype=jnp.int32)[None, :]
    offset = (column - 8 * target).astype(jnp.float32)
    inside = (offset >= 0.0) & (offset < 16.0)
    return jnp.where(inside, (8.0 - jnp.abs(offset - 7.5)) / 64.0, 0.0)


def per_device(scenes, pair_dates, pair_count, inverse):
    slot_count = pair_dates.shape[0]
    looks_here = scenes.shape[3] // 8
    base = lax.all_to_all(scenes, "date", split_axis=2, concat_axis=0, tiled=True)
    used_dates, used_counts = (
        lax.all_gather(pair_dates, "date", axis=0, tiled=True),
        lax.all_gather(pair_count, "date", axis=0, tiled=True),
    )
    slot_index = jnp.arange(used_dates.shape[0], dtype=jnp.int32)
    living = (slot_index % slot_count < jnp.take(used_counts, slot_index // slot_count)).astype(
        jnp.float32
    )
    primary = jnp.take(base, used_dates[:, 0], axis=0)
    secondary = jnp.take(base, used_dates[:, 1], axis=0)
    p_real = primary[:, 0].astype(jnp.float32)
    p_imag = primary[:, 1].astype(jnp.float32)
    s_real = secondary[:, 0].astype(jnp.float32)
    s_imag = secondary[:, 1].astype(jnp.float32)
    real_part = p_real * s_real + p_imag * s_imag
    imaginary = p_imag * s_real - p_real * s_imag
    products = jnp.stack([real_part, imaginary], axis=1) * living[:, None, None, None]
    products = padded(products, (("col", 3),), 4)
    pair_total = products.shape[0]
    padded_width = products.shape[3]
    half_rows = products.shape[2] // 2
    halved = products.reshape(pair_total, 2, half_rows, 2, padded_width).sum(axis=3) * 0.5
    looked = jnp.dot(
        halved.reshape(-1, padded_width),
        look_matrix(padded_width, looks_here),
        precision=lax.Precision.HIGHEST,
        preferred_element_type=jnp.float32,
    )
    looked = looked.reshape(pair_total, 2, half_rows, looks_here)
    return jnp.einsum("qk,kcrm->qcrm", inverse, looked, precision=lax.Precision.HIGHEST)


def solution(mesh):
    placed = (P("date", None, "groups", "col"), P("date", None), P("date"), P())
    return jax.shard_map(
        per_device,
        mesh=mesh,
        in_specs=placed,
        out_specs=P(None, None, ("groups", "date"), "col"),
        check_vma=False,
    )
```

profile of v0, /device:TPU:0, one launch (start us, length us, event | category | flops | bytes accessed | tf_op | source)
XLA Modules:
  0.0 63.4 jit_solution(10447233835666667164)
XLA Ops:
  0.0 0.0 copy-start
  0.0 1.9 %copy.27 = bf16[4,2,64,256]{3,0,1,2:T(4,128)(2,1)} copy(bf16[4,2,64,256]{3,2,1,0:T(8,128)(2,1)} %param.6) | data formatting | bytes 524288 | tf_op args[0]
  1.9 4.2 %all-to-all-start = ((bf16[4,2,64,256]{3,0,1,2:T(4,128)(2,1)}), bf16[4,2,64,256]{3,0,1,2:T(4,128)(2,1)S(1)}, u32[]{:S(2)}, u32[]{:S(2)}) async-start(bf16[4,2,64,256]{3,0,1,2:T(4,128)(2,1)} %copy.27), calls=%async_computation | async-start | bytes 524288 | tf_op jit(solution)/shard_map/all_to_all | solution.py:35
  6.1 6.9 %all-gather = s32[4,24,2]{1,2,0:T(2,128)S(1)} all-gather(s32[1,24,2]{1,2,0:T(2,128)} %bitcast.40), channel_id=1, replica_groups=mesh['groups'=2,'date'=4,'col'=4] {'date'}, dimensions={0}, use_global_device_ids=true | all-gather | bytes 960 | tf_op jit(solution)/shard_map/all_gather | solution.py:37
  13.0 0.1 reshape.140
  13.8 1.2 %dynamic-slice = u32[1]{0:T(128)} dynamic-slice(u32[32]{0:T(128)} %constant.69, u32[]{:T(128)S(6)} %add.68), dynamic_slice_sizes={1} | dynamic-slice | bytes 12
  15.0 0.8 %dynamic-update-slice = s32[4]{0:T(128)S(1)} dynamic-update-slice(s32[4]{0:T(128)S(1)} %broadcast.160, s32[1]{0:T(128)S(6)} %copy.39, u32[]{:T(128)} %bitcast.6) | dynamic-update-slice | bytes 12
  15.8 4.3 %all-reduce = s32[4]{0:T(128)S(1)} all-reduce(s32[4]{0:T(128)S(1)} %dynamic-update-slice), channel_id=1, replica_groups=mesh['groups'=2,'date'=4,'col'=4] {'date'}, use_global_device_ids=true, to_apply=%add | all-reduce | flops 4 | bytes 32
  20.0 0.6 fusion.29
  20.7 2.5 %compare_convert_fusion = f32[96]{0:T(128)S(1)} fusion(s32[]{:T(128)} %bitcast.7, s32[]{:T(128)} %bitcast.8, s32[]{:T(128)} %bitcast.10, s32[]{:T(128)} %bitcast.9), kind=kLoop, calls=%fused_computation.45 | loop fusion | flops 3648 | bytes 400 | tf_op jit(solution)/shard_map/convert_element_type | solution.py:41
  23.2 0.0 all-to-all-done
  23.3 0.7 %gather_fusion = bf16[96,2,16,256]{3,2,1,0:T(8,128)(2,1)S(1)} fusion(bf16[16,2,16,256]{3,2,1,0:T(8,128)(2,1)S(1)} %bitcast.36, s32[1024]{0:T(1024)S(1)} %pad_clamp_fusion.1), kind=kCustom, calls=%fused_computation.clone | custom fusion | bytes 3146112 | tf_op jit(solution)/shard_map/jit(_take)/gather | solution.py:44
  24.0 0.7 %gather_fusion.1 = bf16[96,2,16,256]{3,2,1,0:T(8,128)(2,1)S(1)} fusion(bf16[16,2,16,256]{3,2,1,0:T(8,128)(2,1)S(1)} %bitcast.37, s32[1024]{0:T(1024)S(1)} %pad_clamp_fusion), kind=kCustom, calls=%fused_computation.1.clone | custom fusion | bytes 3146112 | tf_op jit(solution)/shard_map/jit(_take)/gather | solution.py:45
  24.7 0.6 broadcast_select_fusion
  25.3 0.5 fusion.2
  25.8 0.3 maximum_multiply_fusion
  26.1 2.2 %fusion.28 = (f32[96,2,16,4]{3,2,1,0:T(8,128)}, f32[96,2,16,4]{3,2,1,0:T(8,128)}) fusion(f32[96,2,16,256]{3,2,1,0:T(8,128)S(1)} %maximum_multiply_fusion), kind=kLoop, calls=%fused_computation.63 | loop fusion | bytes 196608 | tf_op jit(solution)/shard_map/slice | solution.py:12
  28.3 2.2 %copy.30 = f32[96,2,16,4]{0,2,3,1:T(8,128)S(1)} copy(f32[96,2,16,4]{3,2,1,0:T(8,128)} %get-tuple-element.10) | data formatting | bytes 98304 | tf_op jit(solution)/shard_map/slice | solution.py:12
  30.6 4.1 %collective-permute-start = (f32[96,2,16,4]{0,2,3,1:T(8,128)S(1)}, f32[96,2,16,4]{0,2,3,1:T(8,128)S(1)}, u32[]{:S(2)}, u32[]{:S(2)}) collective-permute-start(f32[96,2,16,4]{0,2,3,1:T(8,128)S(1)} %copy.30), channel_id=1, source_target_pairs={{0,1},{1,2},{2,3},{4,5},{5,6},{6,7},{8,9},{9,10},{10,11},{12,13},{... | collective-permute-start | bytes 147464 | tf_op jit(solution)/shard_map/ppermute | solution.py:15
  34.7 2.2 %copy.31 = f32[96,2,16,4]{0,2,3,1:T(8,128)S(1)} copy(f32[96,2,16,4]{3,2,1,0:T(8,128)} %get-tuple-element.11) | data formatting | bytes 98304 | tf_op jit(solution)/shard_map/slice | solution.py:11
  36.9 1.3 %collective-permute-start.1 = (f32[96,2,16,4]{0,2,3,1:T(8,128)S(1)}, f32[96,2,16,4]{0,2,3,1:T(8,128)S(1)}, u32[]{:S(2)}, u32[]{:S(2)}) collective-permute-start(f32[96,2,16,4]{0,2,3,1:T(8,128)S(1)} %copy.31), channel_id=1, source_target_pairs={{1,0},{2,1},{3,2},{5,4},{6,5},{7,6},{9,8},{10,9},{11,10},{13,12},{... | collective-permute-start | bytes 147464 | tf_op jit(solution)/shard_map/ppermute | solution.py:17
  38.2 0.0 collective-permute-done
  38.2 2.3 %copy.32 = f32[96,2,16,4]{3,2,1,0:T(8,128)} copy(f32[96,2,16,4]{0,2,3,1:T(8,128)S(1)} %collective-permute-done) | data formatting | bytes 98304 | tf_op jit(solution)/shard_map/ppermute | solution.py:15
  40.5 2.5 %collective-permute-done.1 = f32[96,2,16,4]{0,2,3,1:T(8,128)S(1)} collective-permute-done((f32[96,2,16,4]{0,2,3,1:T(8,128)S(1)}, f32[96,2,16,4]{0,2,3,1:T(8,128)S(1)}, u32[]{:S(2)}, u32[]{:S(2)}) %collective-permute-start.1) | collective-permute-done | bytes 49184 | tf_op jit(solution)/shard_map/ppermute | solution.py:17
  43.0 2.4 %copy.33 = f32[96,2,16,4]{3,2,1,0:T(8,128)} copy(f32[96,2,16,4]{0,2,3,1:T(8,128)S(1)} %collective-permute-done.1) | data formatting | bytes 98304 | tf_op jit(solution)/shard_map/ppermute | solution.py:17
  45.4 5.8 %pad_maximum_fusion = f32[96,2,16,264]{3,2,1,0:T(8,128)} fusion(f32[96,2,16,4]{3,2,1,0:T(8,128)} %copy.33, f32[96,2,16,256]{3,2,1,0:T(8,128)S(1)} %maximum_multiply_fusion, f32[96,2,16,4]{3,2,1,0:T(8,128)} %copy.32), kind=kLoop, calls=%fused_computation.2 | loop fusion | flops 1622016 | bytes 6488064 | tf_op jit(solution)/shard_map/concatenate | solution.py:13
  51.2 5.7 %copy.34 = f32[96,2,16,264]{0,3,2,1:T(8,128)} copy(f32[96,2,16,264]{3,2,1,0:T(8,128)} %pad_maximum_fusion) | data formatting | bytes 6488064 | tf_op jit(solution)/shard_map/concatenate | solution.py:13
  57.0 2.8 %reduce_sum.9 = f32[96,2,8,264]{0,3,2,1:T(8,128)S(1)} reduce(f32[96,2,8,2,264]{0,4,3,2,1:T(8,128)} %bitcast.38, f32[]{:T(128)} %constant.55.clone.1), dimensions={3}, to_apply=%region_0.2 | reduce | flops 405504 | bytes 4866052 | tf_op jit(solution)/shard_map/reduce_sum | solution.py:57
  59.8 1.7 %fusion = f32[96,2,8,32]{0,3,2,1:T(8,128)S(1)} fusion(f32[96,2,8,264]{0,3,2,1:T(8,128)S(1)} %reduce_sum.9, s32[32]{0:T(128)S(1)} %iota_multiply_fusion), kind=kOutput, calls=%fused_computation.4 | convolution fusion | flops 156203520 | bytes 1818752 | tf_op jit(solution)/shard_map/dot_general | solution.py:58
  61.6 0.0 copy-done
  61.6 1.1 %convolution_bitcast_fusion = f32[15,2,8,32]{3,0,2,1:T(8,128)S(1)} fusion(f32[96,2,8,32]{0,3,2,1:T(8,128)S(1)} %fusion, f32[15,96]{1,0:T(8,128)S(1)} %copy-done), kind=kOutput, calls=%fused_computation.14 | convolution fusion | flops 8847360 | bytes 233088 | tf_op jit(solution)/shard_map/qk,kcrm->qcrm/dot_general | solution.py:65
  62.7 0.7 %copy.35 = f32[15,2,8,32]{3,2,1,0:T(8,128)} copy(f32[15,2,8,32]{3,0,2,1:T(8,128)S(1)} %convolution_bitcast_fusion) | data formatting | bytes 61440 | tf_op jit(solution)/shard_map/qk,kcrm->qcrm/dot_general | solution.py:65
  (8 shorter events, 0.1 us)
Async XLA Ops:
  0.0 61.6 %copy-start = (f32[15,96]{1,0:T(8,128)S(1)}, f32[15,96]{1,0:T(8,128)}, u32[]{:S(2)}) copy-start(f32[15,96]{1,0:T(8,128)} %param.9) | copy-start | bytes 17284
  1.9 21.3 %all-to-all-start = ((bf16[4,2,64,256]{3,0,1,2:T(4,128)(2,1)}), bf16[4,2,64,256]{3,0,1,2:T(4,128)(2,1)S(1)}, u32[]{:S(2)}, u32[]{:S(2)}) async-start(bf16[4,2,64,256]{3,0,1,2:T(4,128)(2,1)} %copy.27), calls=%async_computation | async-start | bytes 524288 | tf_op jit(solution)/shard_map/all_to_all | solution.py:35
  30.6 7.6 %collective-permute-start = (f32[96,2,16,4]{0,2,3,1:T(8,128)S(1)}, f32[96,2,16,4]{0,2,3,1:T(8,128)S(1)}, u32[]{:S(2)}, u32[]{:S(2)}) collective-permute-start(f32[96,2,16,4]{0,2,3,1:T(8,128)S(1)} %copy.30), channel_id=1, source_target_pairs={{0,1},{1,2},{2,3},{4,5},{5,6},{6,7},{8,9},{9,10},{10,11},{12,13},{... | collective-permute-start | bytes 147464 | tf_op jit(solution)/shard_map/ppermute | solution.py:15
  36.9 6.1 %collective-permute-start.1 = (f32[96,2,16,4]{0,2,3,1:T(8,128)S(1)}, f32[96,2,16,4]{0,2,3,1:T(8,128)S(1)}, u32[]{:S(2)}, u32[]{:S(2)}) collective-permute-start(f32[96,2,16,4]{0,2,3,1:T(8,128)S(1)} %copy.31), channel_id=1, source_target_pairs={{1,0},{2,1},{3,2},{5,4},{6,5},{7,6},{9,8},{10,9},{11,10},{13,12},{... | collective-permute-start | bytes 147464 | tf_op jit(solution)/shard_map/ppermute | solution.py:17
where the time goes:
time: 63.9 us; the launch traced here: 63.4 us
  local copies, waits for them, and re-layouts  23.9 us (37%)
  other arithmetic  12.6 us (20%)
  blocking collectives  11.2 us (18%)
  starting transfers between devices  9.61 us (15%)
  matrix products  2.86 us (4%)
  waiting for transfers between devices  2.51 us (4%)
  between operations  0.79 us (1%)
    all_gather x1, blocking collectives, per_device(): lax.all_gather(pair_dates, 'date', axis=0, tiled=True)  6.89 us
    concatenate x1, other arithmetic, padded(): jnp.concatenate([lax.ppermute(tail, axis, [(i, (i + 1) % count) for i in...  5.82 us
    concatenate x1, local copies, waits for them, and re-layouts, padded(): jnp.concatenate([lax.ppermute(tail, axis, [(i, (i + 1) % count) for i in...  5.75 us
    slice x2, local copies, waits for them, and re-layouts, padded(): lax.slice_in_dim(cells, cells.shape[dim] - width, cells.shape[dim], axis=...  4.45 us
    unnamed x1, blocking collectives  4.29 us
    all_to_all x1, starting transfers between devices, per_device(): lax.all_to_all(scenes, 'date', split_axis=2, concat_axis=0, tiled=True)  4.24 us
    ppermute x1, starting transfers between devices, padded(): lax.ppermute(tail, axis, [(i, (i + 1) % count) for i in range(ends)])  4.09 us
    unnamed x7, local copies, waits for them, and re-layouts  3.95 us
  transfers between devices with their start and end apart: 3, of which 1 were waited for; matrix products, arithmetic and copies ran while one was open for 15% of the time, Pallas kernels for 0%

commit v1 on v0

--- a/solution.py
+++ b/solution.py
@@ -1,7 +1,344 @@
+import functools
+
 import jax
 import jax.numpy as jnp
 from jax import lax
+from jax.experimental import pallas as pl
+from jax.experimental.pallas import tpu as pltpu
 from jax.sharding import PartitionSpec as P
+
+MESH = pl.DeviceIdType.MESH
+F32 = jnp.float32
+BF16 = jnp.bfloat16
+EDGE = 4
+
+
+def flipped(place, slot):
+    bit = 1
+    out = place
+    while bit <= slot:
+        if slot & bit:
+            out = out + bit - 2 * bit * ((place // bit) % 2)
+        bit *= 2
+    return out
+
+
+def split(value):
+    high = value.astype(BF16)
+    return high, (value - high.astype(F32)).astype(BF16)
+
+
+def iota(shape, dim):
+    return lax.broadcasted_iota(jnp.int32, shape, dim)
+
+
+def stack_kernel(
+    cfg,
+    scenes, dates, count, inverse, out,
+    local, base, dates_in, counts_in, edge_out, edge_in,
+    raw, cells, h_high, h_low, weights, k_high, k_low, l_high, l_low,
+    load_sem, send_sem, recv_sem, dates_send, dates_recv, count_send, count_recv, edge_send, edge_recv,
+):
+    D, C, A, R, X, S, NP = (cfg[k] for k in ("D", "C", "A", "R", "X", "S", "NP"))
+    dates_total = D * A
+    T = X // 128
+    TT = T + 1
+    half = R // 2
+    looks = X // 8
+    block = A * A * half
+    diag = block // 2
+    date = lax.axis_index("date")
+    col = lax.axis_index("col")
+    has_left = col > 0
+    has_right = col < C - 1
+
+    load = pltpu.make_async_copy(scenes, local, load_sem)
+    load.start()
+
+    barrier = pltpu.get_barrier_semaphore()
+    for r in range(1, D):
+        pl.semaphore_signal(barrier, inc=1, device_id={"date": flipped(date, r)}, device_id_type=MESH)
+
+    @pl.when(has_left)
+    def _():
+        for r in range(D):
+            pl.semaphore_signal(barrier, inc=1, device_id={"date": flipped(date, r), "col": col - 1}, device_id_type=MESH)
+
+    @pl.when(has_right)
+    def _():
+        for r in range(D):
+            pl.semaphore_signal(barrier, inc=1, device_id={"date": flipped(date, r), "col": col + 1}, device_id_type=MESH)
+
+    load.wait()
+    lane = iota((D * R, 128), 1)
+    to_left = jnp.zeros((D * R, 128), F32)
+    to_right = jnp.zeros((D * R, 128), F32)
+    for i in range(2 * A):
+        first = local[i // 2, i % 2, :, 0:128].astype(F32)
+        last = local[i // 2, i % 2, :, X - 128:X].astype(F32)
+        shift = (8 * i + EDGE) % 128
+        to_left = jnp.where(lane // EDGE == 2 * i + 1, pltpu.roll(first, shift, 1), to_left)
+        shift = (8 * i + EDGE) % 128
+        to_right = jnp.where(lane // EDGE == 2 * i, pltpu.roll(last, shift, 1), to_right)
+    edge_out[0] = to_right.astype(BF16)
+    edge_out[1] = to_left.astype(BF16)
+
+    @pl.when(jnp.logical_not(has_left))
+    def _():
+        edge_in[0] = jnp.zeros((D, R, 128), BF16)
+
+    @pl.when(jnp.logical_not(has_right))
+    def _():
+        edge_in[1] = jnp.zeros((D, R, 128), BF16)
+
+    pl.semaphore_wait(barrier, D - 1 + D * (has_left.astype(jnp.int32) + has_right.astype(jnp.int32)))
+
+    def rows_of(place):
+        return pl.ds(pl.multiple_of(place * R, R), R)
+
+    def remote(src, dst, ssem, rsem, device):
+        return pltpu.make_async_remote_copy(src_ref=src, dst_ref=dst, send_sem=ssem, recv_sem=rsem, device_id=device, device_id_type=MESH)
+
+    to_next = {}
+    order = list(range(D - 1, 0, -1))
+    for r in range(1, D):
+        there = flipped(date, r)
+        to_next["dates", r] = remote(dates, dates_in.at[date], dates_send.at[r], dates_recv.at[r], {"date": there})
+        to_next["count", r] = remote(count, counts_in.at[date], count_send.at[r], count_recv.at[r], {"date": there})
+        to_next["scene", r] = remote(scenes.at[:, :, rows_of(there), :], base.at[r], send_sem.at[r], recv_sem.at[r], {"date": there})
+    for r in range(D):
+        there = flipped(date, r)
+        to_next["right", r] = remote(edge_out.at[0, rows_of(there)], edge_in.at[0, r], edge_send.at[0, r], edge_recv.at[0, r], {"date": there, "col": col + 1})
+        to_next["left", r] = remote(edge_out.at[1, rows_of(there)], edge_in.at[1, r], edge_send.at[1, r], edge_recv.at[1, r], {"date": there, "col": col - 1})
+    for r in order:
+        to_next["dates", r].start()
+        to_next["count", r].start()
+
+    @pl.when(has_right)
+    def _():
+        for r in order + [0]:
+            to_next["right", r].start()
+
+    @pl.when(has_left)
+    def _():
+        for r in order + [0]:
+            to_next["left", r].start()
+
+    for r in cfg["send_order"]:
+        to_next["scene", r].start()
+
+    dates_in[date] = dates[...]
+    counts_in[date] = count[...]
+
+    row = iota((TT * 128, 128), 0)
+    spot = row - TT * 128 + 128
+    column = jnp.where(spot < 0, row, jnp.where(spot < EDGE, spot - EDGE, spot - EDGE + X))
+    usable = (spot < 2 * EDGE)
+    target = iota((TT * 128, 128), 1)
+    for c in range(2):
+        look = target - 64 * c
+        offset = column - 8 * look + 4
+        inside = usable & (look >= 0) & (look < looks) & (offset >= 0) & (offset < 16)
+        value = jnp.where(inside, (8.0 - jnp.abs(offset.astype(F32) - 7.5)) / 128.0, 0.0)
+        weights[c * TT * 128:(c + 1) * TT * 128, :] = value.astype(BF16)
+
+    def unpack(slot, main):
+        for c in range(2):
+            for t in range(T):
+                for i in range(A):
+                    at = ((c * TT + t) * A + i) * R
+                    raw[at:at + R, :] = main(i, c)[:, t * 128:(t + 1) * 128].astype(F32)
+        edges = edge_in[0, slot].astype(F32) + edge_in[1, slot].astype(F32)
+        for c in range(2):
+            for i in range(A):
+                at = ((c * TT + T) * A + i) * R
+                shift = (128 - 8 * (2 * i + c)) % 128
+                raw[at:at + R, :] = pltpu.roll(edges, shift, 1) if shift else edges
+        total = 2 * TT * A * half
+        for parity in range(2):
+            got = raw[pl.ds(parity, total, stride=2), :]
+            cells[parity, :, slot * A:(slot + 1) * A] = got.reshape(2 * TT, A, half, 128)
+
+    def emit(at, pieces):
+        rows = pieces[0][0].shape[0]
+        for t, both in enumerate(pieces):
+            for c in range(2):
+                high, low = split(both[c])
+                h_high[at:at + rows, (c * TT + t) * 128:(c * TT + t + 1) * 128] = high
+                h_low[at:at + rows, (c * TT + t) * 128:(c * TT + t + 1) * 128] = low
+
+    def product(p_of, s_of, t):
+        real = imaginary = None
+        for parity in range(2):
+            p0, p1 = p_of(parity, t), p_of(parity, TT + t)
+            s0, s1 = s_of(parity, t), s_of(parity, TT + t)
+            one = p0 * s0 + p1 * s1
+            two = p1 * s0 - p0 * s1
+            real = one if real is None else real + one
+            imaginary = two if imaginary is None else imaginary + two
+        return real, imaginary
+
+    def pair_order(ra, rb):
+        bit = 1
+        while 2 * bit <= (ra ^ rb):
+            bit *= 2
+        swap = (flipped(date, ra) // bit) % 2
+        low = ra + swap * (rb - ra)
+        high = rb - swap * (rb - ra)
+        return low, high
+
+    chunks = []
+
+    def cross(ra, rb):
+        at = len(chunks) * block
+        chunks.append((ra, rb))
+        low, high = pair_order(ra, rb)
+        for i in range(A):
+            pieces = []
+            for t in range(TT):
+                both = product(
+                    lambda q, n: cells[q, n, low * A + i][None],
+                    lambda q, n: cells[q, n, pl.ds(high * A, A)], t)
+                pieces.append([v.reshape(A * half, 128) for v in both])
+            emit(at + i * A * half, pieces)
+
+    def within(ra):
+        at = len(chunks) * block
+        chunks.append((ra, ra + 1))
+        for side in range(2):
+            slot = ra + side
+            pieces = []
+            for t in range(TT):
+                parts = [], []
+                for step in range(1, A):
+                    both = product(
+                        lambda q, n: cells[q, n, slot * A:slot * A + A - step],
+                        lambda q, n: cells[q, n, slot * A + step:slot * A + A], t)
+                    for c in range(2):
+                        parts[c].append(both[c].reshape((A - step) * half, 128))
+                pad = jnp.zeros((diag - A * (A - 1) // 2 * half, 128), F32)
+                pieces.append([jnp.concatenate(parts[c] + [pad], axis=0) for c in range(2)])
+            emit(at + side * diag, pieces)
+
+    def look(start, stop):
+        rows = slice(start * block, stop * block)
+        got = jnp.dot(h_high[rows, :], weights[...], preferred_element_type=F32)
+        got = got + jnp.dot(h_low[rows, :], weights[...], preferred_element_type=F32)
+        l_high[rows, :], l_low[rows, :] = split(got)
+
+    def wait_edges(r):
+        @pl.when(has_left)
+        def _():
+            to_next["right", r].wait_recv()
+
+        @pl.when(has_right)
+        def _():
+            to_next["left", r].wait_recv()
+
+    wait_edges(0)
+    unpack(0, lambda i, c: local[i, c, rows_of(date), :])
+
+    order_in = cfg["order_in"]
+    looked = 0
+    arrived = [0]
+    for r in order_in:
+        if r == order_in[0]:
+            for q in range(1, D):
+                to_next["dates", q].wait_recv()
+                to_next["count", q].wait_recv()
+        wait_edges(r)
+        to_next["scene", r].wait_recv()
+        unpack(r, lambda i, c: base[r, i, c])
+        if (r ^ 1) in arrived:
+            within(r & ~1)
+        for other in arrived:
+            cross(min(other, r), max(other, r))
+        arrived.append(r)
+        look(looked, len(chunks))
+        looked = len(chunks)
+        if r == order_in[0]:
+            invert_matrix(cfg, date, dates_in, counts_in, inverse, k_high, k_low, pair_order)
+
+    lh, ll = l_high[...], l_low[...]
+    kh = k_high[...]
+    series = jnp.dot(kh, lh, preferred_element_type=F32)
+    series = series + jnp.dot(kh, ll, preferred_element_type=F32)
+    series = series + jnp.dot(k_low[...], lh, preferred_element_type=F32)
+    for c in range(2):
+        out[:, c] = series[:, c * 64:c * 64 + looks].reshape(NP, half, looks)
+
+    for r in range(1, D):
+        for kind in ("dates", "count", "scene"):
+            to_next[kind, r].wait_send()
+
+    @pl.when(has_right)
+    def _():
+        for r in range(D):
+            to_next["right", r].wait_send()
+
+    @pl.when(has_left)
+    def _():
+        for r in range(D):
+            to_next["left", r].wait_send()
+
+
+def chunk_list(order_in):
+    chunks, arrived = [], [0]
+    for r in order_in:
+        if (r ^ 1) in arrived:
+            chunks.append((r & ~1, None))
+        for other in arrived:
+            chunks.append((min(other, r), max(other, r)))
+        arrived.append(r)
+    return chunks
+
+
+def invert_matrix(cfg, date, dates_in, counts_in, inverse, k_high, k_low, pair_order):
+    D, A, R, S, NP = (cfg[k] for k in ("D", "A", "R", "S", "NP"))
+    half = R // 2
+    block = A * A * half
+    diag = block // 2
+    total = D * A
+    codes = []
+    for d in range(D):
+        row = dates_in[d, 0:1, :] * total + dates_in[d, 1:2, :]
+        live = iota((1, S), 1) < counts_in[d]
+        codes.append(jnp.where(live, row, -1).astype(F32))
+    codes.append(jnp.full((8 - D % 8 if D % 8 else 8, S), -1.0, F32))
+    table = jnp.concatenate(codes, axis=0)
+    table = jnp.concatenate([table, jnp.full((table.shape[0], 128 - S), -1.0, F32)], axis=1)
+    turned = jnp.transpose(table)
+    code = jnp.concatenate([turned[0:S, d:d + 1] for d in range(D)], axis=0).astype(jnp.int32)
+    inv = inverse[...]
+    spread = jnp.broadcast_to(inv[:, None, :], (NP, half, D * S)).reshape(NP * half, D * S)
+    spread_high, spread_low = split(spread)
+    place = iota((1, block), 1)
+    same = (iota((NP * half, block), 0) % half) == (iota((NP * half, block), 1) % half)
+    for n, (ra, rb) in enumerate(chunk_list(cfg["order_in"])):
+        if rb is None:
+            slot = place // diag
+            index = (place % diag) // half
+            first = jnp.zeros_like(place)
+            second = jnp.zeros_like(place) - 1
+            at = 0
+            for step in range(1, A):
+                for i in range(A - step):
+                    first = jnp.where(index == at, i, first)
+                    second = jnp.where(index == at, i + step, second)
+                    at += 1
+            owner = jnp.where(slot == 0, flipped(date, ra), flipped(date, ra + 1))
+            want = jnp.where(second >= 0, (owner * A + first) * total + owner * A + second, -2)
+        else:
+            low, high = pair_order(ra, rb)
+            lo_date, hi_date = cfg["place_of"](date, low), cfg["place_of"](date, high)
+            first = lo_date * A + place // (A * half)
+            second = hi_date * A + (place // half) % A
+            want = first * total + second
+        hit = jnp.where(code == want, 1.0, 0.0).astype(BF16)
+        value = jnp.dot(spread_high, hit, preferred_element_type=F32) + jnp.dot(spread_low, hit, preferred_element_type=F32)
+        value = jnp.where(same, value, 0.0)
+        columns = slice(n * block, (n + 1) * block)
+        k_high[:, columns], k_low[:, columns] = split(value)
 
 
 def padded(cells, sides, width):
@@ -29,7 +366,7 @@
     return jnp.where(inside, (8.0 - jnp.abs(offset - 7.5)) / 64.0, 0.0)
 
 
-def per_device(scenes, pair_dates, pair_count, inverse):
+def plain_device(scenes, pair_dates, pair_count, inverse):
     slot_count = pair_dates.shape[0]
     looks_here = scenes.shape[3] // 8
     base = lax.all_to_all(scenes, "date", split_axis=2, concat_axis=0, tiled=True)
@@ -65,6 +402,61 @@
     return jnp.einsum("qk,kcrm->qcrm", inverse, looked, precision=lax.Precision.HIGHEST)
 
 
+def per_device(scenes, pair_dates, pair_count, inverse):
+    D, C = lax.axis_size("date"), lax.axis_size("col")
+    A, _, rows, X = scenes.shape
+    S, NP = pair_dates.shape[0], inverse.shape[0]
+    R = rows // D
+    half = R // 2
+    block = A * A * half
+    fits = R % 16 == 0 and X % 128 == 0 and X // 8 <= 64 and D & (D - 1) == 0 and 1 < D and S % 8 == 0 and S <= 128
+    fits = fits and block % 128 == 0 and A * (A - 1) // 2 * half <= block // 2 and (block // 2) % 16 == 0 and 8 * 2 * A <= 128
+    if not fits or D > 8:
+        return plain_device(scenes, pair_dates, pair_count, inverse)
+    order_in = list(range(1, D))
+    cfg = dict(D=D, C=C, A=A, R=R, X=X, S=S, NP=NP, order_in=order_in, send_order=order_in, place_of=place_of(D))
+    total = len(chunk_list(order_in)) * block
+    TT = X // 128 + 1
+    dma = pltpu.SemaphoreType.DMA
+    vmem = pl.BlockSpec(memory_space=pltpu.VMEM)
+    return pl.pallas_call(
+        functools.partial(stack_kernel, cfg),
+        out_shape=jax.ShapeDtypeStruct((NP, 2, half, X // 8), F32),
+        in_specs=[pl.BlockSpec(memory_space=pl.ANY), vmem, vmem, vmem],
+        out_specs=vmem,
+        scratch_shapes=[
+            pltpu.VMEM(scenes.shape, BF16),
+            pltpu.VMEM((D, A, 2, R, X), BF16),
+            pltpu.VMEM((D, 2, S), jnp.int32),
+            pltpu.VMEM((D, 1, 1), jnp.int32),
+            pltpu.VMEM((2, rows, 128), BF16),
+            pltpu.VMEM((2, D, R, 128), BF16),
+            pltpu.VMEM((2 * TT * A * R, 128), F32),
+            pltpu.VMEM((2, 2 * TT, D * A, half, 128), F32),
+            pltpu.VMEM((total, 2 * TT * 128), BF16),
+            pltpu.VMEM((total, 2 * TT * 128), BF16),
+            pltpu.VMEM((2 * TT * 128, 128), BF16),
+            pltpu.VMEM((NP * half, total), BF16),
+            pltpu.VMEM((NP * half, total), BF16),
+            pltpu.VMEM((total, 128), BF16),
+            pltpu.VMEM((total, 128), BF16),
+            dma, dma((D,)), dma((D,)), dma((D,)), dma((D,)), dma((D,)), dma((D,)), dma((2, D)), dma((2, D)),
+        ],
+        compiler_params=pltpu.CompilerParams(collective_id=0, has_side_effects=True),
+    )(scenes, pair_dates.T, pair_count.reshape(1, 1), inverse)
+
+
+def place_of(D):
+    def combine(place, slot):
+        out, bit = 0, 1
+        while bit < D:
+            a, b = (place // bit) % 2, (slot // bit) % 2
+            out = out + bit * (a + b - 2 * a * b)
+            bit *= 2
+        return out
+    return combine
+
+
 def solution(mesh):
     placed = (P("date", None, "groups", "col"), P("date", None), P("date"), P())
     return jax.shard_map(

time: 63.9 us -> 15 us (0.23)
  local copies, waits for them, and re-layouts: 23.9 us -> 1.56 us
  Pallas kernels: 0 us -> 12.6 us
  other arithmetic: 12.6 us -> 0 us
  blocking collectives: 11.2 us -> 0 us
  starting transfers between devices: 9.61 us -> 0 us
  matrix products: 2.86 us -> 0 us
  waiting for transfers between devices: 2.51 us -> 0 us
    pallas_call x0 -> x1, Pallas kernels: none -> 12.6 us  [per_device(): pl.pallas_call(functools.partial(stack_kernel, cfg), out_shape=jax.ShapeD...]
    all_gather x1 -> x0, blocking collectives: 6.89 us -> none  [per_device(): lax.all_gather(pair_dates, 'date', axis=0, tiled=True)]
    slice x3 -> x0, local copies, waits for them, and re-layouts: 6.68 us -> none  [the longest x2 4.45 us: padded(): lax.slice_in_dim(cells, cells.shape[dim] - width, cells.shape[dim], axis=...]
    concatenate x1 -> x0, other arithmetic: 5.82 us -> none  [padded(): jnp.concatenate([lax.ppermute(tail, axis, [(i, (i + 1) % count) for i in...]
    concatenate x1 -> x0, local copies, waits for them, and re-layouts: 5.75 us -> none  [padded(): jnp.concatenate([lax.ppermute(tail, axis, [(i, (i + 1) % count) for i in...]
    ppermute x2 -> x0, starting transfers between devices: 5.37 us -> none  [the longest x1 4.09 us: padded(): lax.ppermute(tail, axis, [(i, (i + 1) % count) for i in range(ends)])]
    ppermute x2 -> x0, local copies, waits for them, and re-layouts: 4.69 us -> none  [the longest x1 2.36 us: padded(): lax.ppermute(head, axis, [((i + 1) % count, i) for i in range(ends)])]
    unnamed x1 -> x0, blocking collectives: 4.29 us -> none
  transfers between devices with their start and end apart: 3 -> 0, of which waited for: 1 -> 0; matrix products, arithmetic and copies ran while one was open for 15% -> 0% of each run, Pallas kernels for 0% -> 0%
where the time goes in v1:
time: 15 us; the launch traced here: 14.8 us
  Pallas kernels  12.6 us (84%)
  local copies, waits for them, and re-layouts  1.56 us (10%)
  between operations  0.66 us (4%)
    pallas_call x1, Pallas kernels, per_device(): pl.pallas_call(functools.partial(stack_kernel, cfg), out_shape=jax.ShapeD...  12.6 us
    unnamed x1, local copies, waits for them, and re-layouts  1.56 us

profile of v1, /device:TPU:0, one launch (start us, length us, event | category | flops | bytes accessed | tf_op | source)
XLA Modules:
  0.0 14.8 jit_solution(17272769802012112605)
XLA Ops:
  0.7 12.6 %shard_map.46 = f32[15,2,8,32]{3,2,1,0:T(8,128)} custom-call(bf16[4,2,64,256]{3,2,1,0:T(8,128)(2,1)} %scenes.1, s32[2,24]{1,0:T(2,128)} %bitcast.3, s32[1,1]{1,0:T(1,128)} %bitcast.2.count, f32[15,96]{1,0:T(8,128)} %inverse.1), custom_call_target="tpu_custom_call" | custom-call | tf_op jit(solution)/shard_map/pallas_call | solution.py:422
  13.2 1.6 %copy.7 = f32[15,2,8,32]{3,2,1,0:T(8,128)} copy(f32[15,2,8,32]{3,2,1,0:T(8,128)} %shard_map.46) | data formatting | bytes 61440

commit v2 on v1

--- a/solution.py
+++ b/solution.py
@@ -38,6 +38,7 @@
     local, base, dates_in, counts_in, edge_out, edge_in,
     raw, cells, h_high, h_low, weights, k_high, k_low, l_high, l_low,
     load_sem, send_sem, recv_sem, dates_send, dates_recv, count_send, count_recv, edge_send, edge_recv,
+    inverse_in, own_sem,
 ):
     D, C, A, R, X, S, NP = (cfg[k] for k in ("D", "C", "A", "R", "X", "S", "NP"))
     dates_total = D * A
@@ -52,9 +53,6 @@
     has_left = col > 0
     has_right = col < C - 1
 
-    load = pltpu.make_async_copy(scenes, local, load_sem)
-    load.start()
-
     barrier = pltpu.get_barrier_semaphore()
     for r in range(1, D):
         pl.semaphore_signal(barrier, inc=1, device_id={"date": flipped(date, r)}, device_id_type=MESH)
@@ -68,6 +66,17 @@
     def _():
         for r in range(D):
             pl.semaphore_signal(barrier, inc=1, device_id={"date": flipped(date, r), "col": col + 1}, device_id_type=MESH)
+
+    load = pltpu.make_async_copy(scenes, local, load_sem)
+    load.start()
+    own = [
+        pltpu.make_async_copy(dates, dates_in.at[date], own_sem.at[0]),
+        pltpu.make_async_copy(count, counts_in.at[date], own_sem.at[1]),
+        pltpu.make_async_copy(inverse, inverse_in, own_sem.at[2]),
+    ]
+
+    for copy in own:
+        copy.start()
 
     load.wait()
     lane = iota((D * R, 128), 1)
@@ -126,9 +135,6 @@
 
     for r in cfg["send_order"]:
         to_next["scene", r].start()
-
-    dates_in[date] = dates[...]
-    counts_in[date] = count[...]
 
     row = iota((TT * 128, 128), 0)
     spot = row - TT * 128 + 128
@@ -243,6 +249,8 @@
     arrived = [0]
     for r in order_in:
         if r == order_in[0]:
+            for copy in own:
+                copy.wait()
             for q in range(1, D):
                 to_next["dates", q].wait_recv()
                 to_next["count", q].wait_recv()
@@ -257,7 +265,7 @@
         look(looked, len(chunks))
         looked = len(chunks)
         if r == order_in[0]:
-            invert_matrix(cfg, date, dates_in, counts_in, inverse, k_high, k_low, pair_order)
+            invert_matrix(cfg, date, dates_in, counts_in, inverse_in, k_high, k_low, pair_order)
 
     lh, ll = l_high[...], l_low[...]
     kh = k_high[...]
@@ -421,8 +429,8 @@
     vmem = pl.BlockSpec(memory_space=pltpu.VMEM)
     return pl.pallas_call(
         functools.partial(stack_kernel, cfg),
-        out_shape=jax.ShapeDtypeStruct((NP, 2, half, X // 8), F32),
-        in_specs=[pl.BlockSpec(memory_space=pl.ANY), vmem, vmem, vmem],
+        out_shape=pltpu.VMEM((NP, 2, half, X // 8), F32),
+        in_specs=[pl.BlockSpec(memory_space=pltpu.HBM)] * 4,
         out_specs=vmem,
         scratch_shapes=[
             pltpu.VMEM(scenes.shape, BF16),
@@ -441,6 +449,7 @@
             pltpu.VMEM((total, 128), BF16),
             pltpu.VMEM((total, 128), BF16),
             dma, dma((D,)), dma((D,)), dma((D,)), dma((D,)), dma((D,)), dma((D,)), dma((2, D)), dma((2, D)),
+            pltpu.VMEM(inverse.shape, F32), dma((3,)),
         ],
         compiler_params=pltpu.CompilerParams(collective_id=0, has_side_effects=True),
     )(scenes, pair_dates.T, pair_count.reshape(1, 1), inverse)

time: 15 us -> 12.8 us (0.85)
  Pallas kernels: 12.6 us -> 11.3 us
  local copies, waits for them, and re-layouts: 1.56 us -> 0.65 us
    pallas_call x1, Pallas kernels: 12.6 us -> 11.3 us  [per_device(): pl.pallas_call(functools.partial(stack_kernel, cfg), out_shape=pltpu.VMEM...]
    unnamed x1, local copies, waits for them, and re-layouts: 1.56 us -> 0.65 us
where the time goes in v2:
time: 12.8 us; the launch traced here: 12.6 us
  Pallas kernels  11.3 us (88%)
  between operations  0.66 us (5%)
  local copies, waits for them, and re-layouts  0.65 us (5%)
    pallas_call x1, Pallas kernels, per_device(): pl.pallas_call(functools.partial(stack_kernel, cfg), out_shape=pltpu.VMEM...  11.3 us
    unnamed x1, local copies, waits for them, and re-layouts  0.65 us

profile of v2, /device:TPU:0, one launch (start us, length us, event | category | flops | bytes accessed | tf_op | source)
XLA Modules:
  0.0 12.6 jit_solution(11873960463904168398)
XLA Ops:
  0.7 11.3 %shard_map.46 = f32[15,2,8,32]{3,2,1,0:T(8,128)S(1)} custom-call(bf16[4,2,64,256]{3,2,1,0:T(8,128)(2,1)} %scenes.1, s32[2,24]{1,0:T(2,128)} %bitcast.3, s32[1,1]{1,0:T(1,128)} %bitcast.2.count, f32[15,96]{1,0:T(8,128)} %inverse.1), custom_call_target="tpu_custom_call" | custom-call | tf_op jit(solution)/shard_map/pallas_call | solution.py:430
  12.0 0.7 %copy.6 = f32[15,2,8,32]{3,2,1,0:T(8,128)} copy(f32[15,2,8,32]{3,2,1,0:T(8,128)S(1)} %shard_map.46) | data formatting | bytes 61440

commit v3 on v0

--- a/solution.py
+++ b/solution.py
@@ -1,7 +1,349 @@
+import functools
+
 import jax
 import jax.numpy as jnp
 from jax import lax
+from jax.experimental import pallas as pl
+from jax.experimental.pallas import tpu as pltpu
 from jax.sharding import PartitionSpec as P
+
+MESH = pl.DeviceIdType.MESH
+F32 = jnp.float32
+BF16 = jnp.bfloat16
+EDGE = 4
+
+
+def flipped(place, slot):
+    bit = 1
+    out = place
+    while bit <= slot:
+        if slot & bit:
+            out = out + bit - 2 * bit * ((place // bit) % 2)
+        bit *= 2
+    return out
+
+
+def split(value):
+    high = value.astype(BF16)
+    return high, (value - high.astype(F32)).astype(BF16)
+
+
+def iota(shape, dim):
+    return lax.broadcasted_iota(jnp.int32, shape, dim)
+
+
+def stack_kernel(
+    cfg,
+    scenes, dates, count, inverse, out,
+    local, base, dates_in, counts_in, edge_out, edge_in,
+    raw, cells, total, h_high, h_low, weights, k_high, k_low, l_high, l_low,
+    load_sem, send_sem, recv_sem, dates_send, dates_recv, count_send, count_recv, edge_send, edge_recv,
+    inverse_in, own_sem, edge_near, near_send, near_recv,
+):
+    D, C, A, R, X, S, NP = (cfg[k] for k in ("D", "C", "A", "R", "X", "S", "NP"))
+    T = X // 128
+    TT = T + 1
+    half = R // 2
+    looks = X // 8
+    date = lax.axis_index("date")
+    col = lax.axis_index("col")
+    has_left = col > 0
+    has_right = col < C - 1
+
+    barrier = pltpu.get_barrier_semaphore()
+    for r in range(1, D):
+        pl.semaphore_signal(barrier, inc=1, device_id={"date": flipped(date, r)}, device_id_type=MESH)
+
+    @pl.when(has_left)
+    def _():
+        pl.semaphore_signal(barrier, inc=1, device_id={"col": col - 1}, device_id_type=MESH)
+
+    @pl.when(has_right)
+    def _():
+        pl.semaphore_signal(barrier, inc=1, device_id={"col": col + 1}, device_id_type=MESH)
+
+    load = pltpu.make_async_copy(scenes, local, load_sem)
+    load.start()
+    own = [
+        pltpu.make_async_copy(dates, dates_in.at[date], own_sem.at[0]),
+        pltpu.make_async_copy(count, counts_in.at[date], own_sem.at[1]),
+        pltpu.make_async_copy(inverse, inverse_in, own_sem.at[2]),
+    ]
+
+    for copy in own:
+        copy.start()
+
+    load.wait()
+    lane = iota((D * R, 128), 1)
+    to_left = jnp.zeros((D * R, 128), F32)
+    to_right = jnp.zeros((D * R, 128), F32)
+    for i in range(2 * A):
+        first = local[i // 2, i % 2, :, 0:128].astype(F32)
+        last = local[i // 2, i % 2, :, X - 128:X].astype(F32)
+        shift = (8 * i + EDGE) % 128
+        to_left = jnp.where(lane // EDGE == 2 * i + 1, pltpu.roll(first, shift, 1), to_left)
+        shift = (8 * i + EDGE) % 128
+        to_right = jnp.where(lane // EDGE == 2 * i, pltpu.roll(last, shift, 1), to_right)
+    edge_out[0] = to_right.astype(BF16)
+    edge_out[1] = to_left.astype(BF16)
+
+    for side, present in ((0, has_left), (1, has_right)):
+        @pl.when(jnp.logical_not(present))
+        def _():
+            edge_in[side] = jnp.zeros((D, R, 128), BF16)
+            edge_near[side] = jnp.zeros((D * R, 128), BF16)
+
+    pl.semaphore_wait(barrier, D - 1 + (has_left.astype(jnp.int32) + has_right.astype(jnp.int32)))
+
+    def rows_of(place):
+        return pl.ds(pl.multiple_of(place * R, R), R)
+
+    def remote(src, dst, ssem, rsem, device):
+        return pltpu.make_async_remote_copy(src_ref=src, dst_ref=dst, send_sem=ssem, recv_sem=rsem, device_id=device, device_id_type=MESH)
+
+    to_next = {}
+    order = list(range(D - 1, 0, -1))
+    for r in range(1, D):
+        there = flipped(date, r)
+        to_next["dates", r] = remote(dates, dates_in.at[date], dates_send.at[r], dates_recv.at[r], {"date": there})
+        to_next["count", r] = remote(count, counts_in.at[date], count_send.at[r], count_recv.at[r], {"date": there})
+        for begin, end in cfg["cuts"][r]:
+            to_next["scene", r, begin] = remote(
+                scenes.at[begin:end, :, rows_of(there), :], base.at[r, begin:end],
+                send_sem.at[r, begin], recv_sem.at[r, begin], {"date": there})
+    near = (
+        remote(edge_out.at[0], edge_near.at[0], near_send.at[0], near_recv.at[0], {"col": col + 1}),
+        remote(edge_out.at[1], edge_near.at[1], near_send.at[1], near_recv.at[1], {"col": col - 1}),
+    )
+    for r in range(1, D):
+        there = flipped(date, r)
+        for side in range(2):
+            to_next["edge", side, r] = remote(edge_near.at[side, rows_of(there)], edge_in.at[side, r], edge_send.at[side, r], edge_recv.at[side, r], {"date": there})
+
+    @pl.when(has_right)
+    def _():
+        near[0].start()
+
+    @pl.when(has_left)
+    def _():
+        near[1].start()
+
+    order_in = cfg["order_in"]
+    early = [r for r in order_in if r <= D // 2]
+    late = [r for r in order_in if r > D // 2]
+    for r in order_in[::-1]:
+        to_next["dates", r].start()
+        to_next["count", r].start()
+    for r in early:
+        for begin, _ in cfg["cuts"][r]:
+            to_next["scene", r, begin].start()
+
+    row = iota((TT * 128, 128), 0)
+    spot = row - TT * 128 + 128
+    column = jnp.where(spot < 0, row, jnp.where(spot < EDGE, spot - EDGE, spot - EDGE + X))
+    usable = (spot < 2 * EDGE)
+    target = iota((TT * 128, 128), 1)
+    for c in range(2):
+        look = target - 64 * c
+        offset = column - 8 * look + 4
+        inside = usable & (look >= 0) & (look < looks) & (offset >= 0) & (offset < 16)
+        value = jnp.where(inside, (8.0 - jnp.abs(offset.astype(F32) - 7.5)) / 128.0, 0.0)
+        weights[c * TT * 128:(c + 1) * TT * 128, :] = value.astype(BF16)
+
+    for side, present in ((0, has_left), (1, has_right)):
+        @pl.when(present)
+        def _():
+            near[side].wait_recv()
+            for r in order_in[::-1]:
+                to_next["edge", side, r].start()
+
+    for r in late:
+        for begin, _ in cfg["cuts"][r]:
+            to_next["scene", r, begin].start()
+
+    def unpack(slot, begin, end, main):
+        many = end - begin
+        for c in range(2):
+            for t in range(T):
+                for i in range(many):
+                    at = ((c * TT + t) * many + i) * R
+                    raw[at:at + R, :] = main(begin + i, c)[:, t * 128:(t + 1) * 128].astype(F32)
+        at_edge = [edge_in[n, slot] if slot else edge_near[n, rows_of(date), :] for n in range(2)]
+        edges = at_edge[0].astype(F32) + at_edge[1].astype(F32)
+        for c in range(2):
+            for i in range(many):
+                at = ((c * TT + T) * many + i) * R
+                shift = (128 - 8 * (2 * (begin + i) + c)) % 128
+                raw[at:at + R, :] = pltpu.roll(edges, shift, 1) if shift else edges
+        size = 2 * TT * many * half
+        for parity in range(2):
+            got = raw[pl.ds(parity, size, stride=2), :]
+            cells[parity, :, slot * A + begin:slot * A + end] = got.reshape(2 * TT, many, half, 128)
+
+    def wait_edges(r):
+        for side, present in ((0, has_left), (1, has_right)):
+            @pl.when(present)
+            def _():
+                to_next["edge", side, r].wait_recv()
+
+    def product(p_at, s_at, t):
+        real = imaginary = None
+        for parity in range(2):
+            p0, p1 = cells[parity, t, p_at][None], cells[parity, TT + t, p_at][None]
+            s0, s1 = cells[parity, t, s_at], cells[parity, TT + t, s_at]
+            one = p0 * s0 + p1 * s1
+            two = p1 * s0 - p0 * s1
+            real = one if real is None else real + one
+            imaginary = two if imaginary is None else imaginary + two
+        return real, imaginary
+
+    lanes = iota((1, 128), 1)
+
+    def multiply(stage):
+        at = stage["at"]
+        rows = stage["rows"]
+        for t in range(TT):
+            for c in range(2):
+                where = (c * TT + t) * 128
+                parts = []
+                for r, j, q, n, _ in stage["pieces"]:
+                    if c == 0:
+                        made[r, j, q, t] = product(r * A + j, slice(q * A, q * A + n), t)
+                    parts.append(made[r, j, q, t][c].reshape(n * half, 128))
+                if rows > stage["used"]:
+                    parts.append(jnp.zeros((rows - stage["used"], 128), F32))
+                high, low = split(jnp.concatenate(parts, axis=0))
+                h_high[at:at + rows, where:where + 128] = high
+                h_low[at:at + rows, where:where + 128] = low
+        got = jnp.dot(h_high[at:at + rows, :], weights[...], preferred_element_type=F32)
+        got = got + jnp.dot(h_low[at:at + rows, :], weights[...], preferred_element_type=F32)
+        signed = []
+        for r, j, q, n, start in stage["pieces"]:
+            sign = (2 * swapped(date, q, r) - 1).astype(F32) if q != r else -1.0
+            signed.append(got[start:start + n * half] * jnp.where(lanes < 64, 1.0, sign))
+        if rows > stage["used"]:
+            signed.append(got[stage["used"]:rows])
+        l_high[at:at + rows, :], l_low[at:at + rows, :] = split(jnp.concatenate(signed, axis=0))
+
+    made = {}
+
+    def invert(start, stop):
+        rows = slice(start, stop)
+        lh, ll = l_high[rows, :], l_low[rows, :]
+        kh = k_high[:, rows]
+        part = jnp.dot(kh, lh, preferred_element_type=F32)
+        part = part + jnp.dot(kh, ll, preferred_element_type=F32)
+        return part + jnp.dot(k_low[:, rows], lh, preferred_element_type=F32)
+
+    stages = cfg["stages"]
+    for stage in stages:
+        if stage["padded"] > stage["rows"]:
+            gap = slice(stage["at"] + stage["rows"], stage["at"] + stage["padded"])
+            l_high[gap, :] = jnp.zeros((stage["padded"] - stage["rows"], 128), BF16)
+            l_low[gap, :] = jnp.zeros((stage["padded"] - stage["rows"], 128), BF16)
+
+    unpack(0, 0, A, lambda i, c: local[i, c, rows_of(date), :])
+    for copy in own:
+        copy.wait()
+    for q in range(1, D):
+        to_next["dates", q].wait_recv()
+        to_next["count", q].wait_recv()
+    invert_matrix(cfg, date, dates_in, counts_in, inverse_in, k_high, k_low)
+
+    for n, stage in enumerate(stages):
+        for r, begin, end in stage["arrive"]:
+            if begin == 0:
+                wait_edges(r)
+            to_next["scene", r, begin].wait_recv()
+            unpack(r, begin, end, lambda i, c: base[r, i, c])
+        multiply(stage)
+        if n == len(stages) - 2:
+            total[...] = invert(0, stage["at"] + stage["padded"])
+    series = invert(stages[-1]["at"], stages[-1]["at"] + stages[-1]["padded"])
+    if len(stages) > 1:
+        series = series + total[...]
+    for c in range(2):
+        out[:, c] = series[:, c * 64:c * 64 + looks].reshape(NP, half, looks)
+
+    for key, copy in to_next.items():
+        if key[0] in ("dates", "count", "scene"):
+            copy.wait_send()
+
+    for side, come, go in ((0, has_left, has_right), (1, has_right, has_left)):
+        @pl.when(go)
+        def _():
+            near[side].wait_send()
+
+        @pl.when(come)
+        def _():
+            for r in range(1, D):
+                to_next["edge", side, r].wait_send()
+
+
+def swapped(date, low, high):
+    bit = 1
+    while 2 * bit <= (low ^ high):
+        bit *= 2
+    return (flipped(date, low) // bit) % 2
+
+
+def plan(D, A, half):
+    cuts = {r: [(0, A)] for r in range(1, D)}
+    cuts[D - 1] = [(0, A // 2), (A // 2, A)] if A > 1 else [(0, A)]
+    stages, at = [], 0
+    for r in range(1, D):
+        for begin, end in cuts[r]:
+            news = [(r, j) for j in range(begin, end)]
+            if r == 1 and begin == 0:
+                news = [(0, j) for j in range(A)] + news
+            pieces, used = [], 0
+            for slot, j in news:
+                for q in range(slot + 1):
+                    n = A if q < slot else j
+                    if n:
+                        pieces.append((slot, j, q, n, used))
+                        used += n * half
+            rows = -(-used // 16) * 16
+            padded = -(-used // 128) * 128
+            stages.append(dict(arrive=[(r, begin, end)], pieces=pieces, used=used, rows=rows, padded=padded, at=at))
+            at += padded
+    return cuts, stages, at
+
+
+def invert_matrix(cfg, date, dates_in, counts_in, inverse, k_high, k_low):
+    D, A, R, S, NP = (cfg[k] for k in ("D", "A", "R", "S", "NP"))
+    half = R // 2
+    total = D * A
+    codes = []
+    for d in range(D):
+        row = dates_in[d, 0:1, :] * total + dates_in[d, 1:2, :]
+        live = iota((1, S), 1) < counts_in[d]
+        codes.append(jnp.where(live, row, -1).astype(F32))
+    codes.append(jnp.full((8 - D % 8 if D % 8 else 8, S), -1.0, F32))
+    table = jnp.concatenate(codes, axis=0)
+    table = jnp.concatenate([table, jnp.full((table.shape[0], 128 - S), -1.0, F32)], axis=1)
+    turned = jnp.transpose(table)
+    code = jnp.concatenate([turned[0:S, d:d + 1] for d in range(D)], axis=0).astype(jnp.int32)
+    inv = inverse[...]
+    spread = jnp.broadcast_to(inv[:, None, :], (NP, half, D * S)).reshape(NP * half, D * S)
+    spread_high, spread_low = split(spread)
+    for stage in cfg["stages"]:
+        width = stage["padded"]
+        place = iota((1, width), 1)
+        same = (iota((NP * half, width), 0) % half) == (iota((NP * half, width), 1) % half)
+        want = jnp.full((1, width), -2, jnp.int32)
+        for r, j, q, n, start in stage["pieces"]:
+            new, old = flipped(date, r) * A + j, flipped(date, q) * A
+            swap = swapped(date, q, r) if q != r else 0
+            first = swap * (new * total + old) + (1 - swap) * (old * total + new)
+            step = swap + (1 - swap) * total
+            inside = (place >= start) & (place < start + n * half)
+            want = jnp.where(inside, first + step * ((place - start) // half), want)
+        hit = jnp.where(code == want, 1.0, 0.0).astype(BF16)
+        value = jnp.dot(spread_high, hit, preferred_element_type=F32) + jnp.dot(spread_low, hit, preferred_element_type=F32)
+        value = jnp.where(same, value, 0.0)
+        columns = slice(stage["at"], stage["at"] + width)
+        k_high[:, columns], k_low[:, columns] = split(value)
 
 
 def padded(cells, sides, width):
@@ -29,7 +371,7 @@
     return jnp.where(inside, (8.0 - jnp.abs(offset - 7.5)) / 64.0, 0.0)
 
 
-def per_device(scenes, pair_dates, pair_count, inverse):
+def plain_device(scenes, pair_dates, pair_count, inverse):
     slot_count = pair_dates.shape[0]
     looks_here = scenes.shape[3] // 8
     base = lax.all_to_all(scenes, "date", split_axis=2, concat_axis=0, tiled=True)
@@ -65,6 +407,50 @@
     return jnp.einsum("qk,kcrm->qcrm", inverse, looked, precision=lax.Precision.HIGHEST)
 
 
+def per_device(scenes, pair_dates, pair_count, inverse):
+    D, C = lax.axis_size("date"), lax.axis_size("col")
+    A, _, rows, X = scenes.shape
+    S, NP = pair_dates.shape[0], inverse.shape[0]
+    R = rows // D
+    half = R // 2
+    fits = R % 16 == 0 and X % 128 == 0 and X // 8 <= 64 and D & (D - 1) == 0 and 1 < D <= 8
+    fits = fits and S % 8 == 0 and S <= 128 and 16 * A <= 128
+    if not fits:
+        return plain_device(scenes, pair_dates, pair_count, inverse)
+    cuts, stages, total = plan(D, A, half)
+    cfg = dict(D=D, C=C, A=A, R=R, X=X, S=S, NP=NP, order_in=list(range(1, D)), cuts=cuts, stages=stages)
+    TT = X // 128 + 1
+    dma = pltpu.SemaphoreType.DMA
+    vmem = pl.BlockSpec(memory_space=pltpu.VMEM)
+    return pl.pallas_call(
+        functools.partial(stack_kernel, cfg),
+        out_shape=pltpu.VMEM((NP, 2, half, X // 8), F32),
+        in_specs=[pl.BlockSpec(memory_space=pltpu.HBM)] * 4,
+        out_specs=vmem,
+        scratch_shapes=[
+            pltpu.VMEM(scenes.shape, BF16),
+            pltpu.VMEM((D, A, 2, R, X), BF16),
+            pltpu.VMEM((D, 2, S), jnp.int32),
+            pltpu.VMEM((D, 1, 1), jnp.int32),
+            pltpu.VMEM((2, rows, 128), BF16),
+            pltpu.VMEM((2, D, R, 128), BF16),
+            pltpu.VMEM((2 * TT * A * R, 128), F32),
+            pltpu.VMEM((2, 2 * TT, D * A, half, 128), F32),
+            pltpu.VMEM((NP * half, 128), F32),
+            pltpu.VMEM((total, 2 * TT * 128), BF16),
+            pltpu.VMEM((total, 2 * TT * 128), BF16),
+            pltpu.VMEM((2 * TT * 128, 128), BF16),
+            pltpu.VMEM((NP * half, total), BF16),
+            pltpu.VMEM((NP * half, total), BF16),
+            pltpu.VMEM((total, 128), BF16),
+            pltpu.VMEM((total, 128), BF16),
+            dma, dma((D, A)), dma((D, A)), dma((D,)), dma((D,)), dma((D,)), dma((D,)), dma((2, D)), dma((2, D)),
+            pltpu.VMEM(inverse.shape, F32), dma((3,)), pltpu.VMEM((2, rows, 128), BF16), dma((2,)), dma((2,)),
+        ],
+        compiler_params=pltpu.CompilerParams(collective_id=0, has_side_effects=True),
+    )(scenes, pair_dates.T, pair_count.reshape(1, 1), inverse)
+
+
 def solution(mesh):
     placed = (P("date", None, "groups", "col"), P("date", None), P("date"), P())
     return jax.shard_map(

time: 63.9 us -> 14.5 us (0.23)
  local copies, waits for them, and re-layouts: 23.9 us -> 0.65 us
  Pallas kernels: 0 us -> 13 us
  other arithmetic: 12.6 us -> 0 us
  blocking collectives: 11.2 us -> 0 us
  starting transfers between devices: 9.61 us -> 0 us
  matrix products: 2.86 us -> 0 us
  waiting for transfers between devices: 2.51 us -> 0 us
    pallas_call x0 -> x1, Pallas kernels: none -> 13 us  [per_device(): pl.pallas_call(functools.partial(stack_kernel, cfg), out_shape=pltpu.VMEM...]
    all_gather x1 -> x0, blocking collectives: 6.89 us -> none  [per_device(): lax.all_gather(pair_dates, 'date', axis=0, tiled=True)]
    slice x3 -> x0, local copies, waits for them, and re-layouts: 6.68 us -> none  [the longest x2 4.45 us: padded(): lax.slice_in_dim(cells, cells.shape[dim] - width, cells.shape[dim], axis=...]
    concatenate x1 -> x0, other arithmetic: 5.82 us -> none  [padded(): jnp.concatenate([lax.ppermute(tail, axis, [(i, (i + 1) % count) for i in...]
    concatenate x1 -> x0, local copies, waits for them, and re-layouts: 5.75 us -> none  [padded(): jnp.concatenate([lax.ppermute(tail, axis, [(i, (i + 1) % count) for i in...]
    ppermute x2 -> x0, starting transfers between devices: 5.37 us -> none  [the longest x1 4.09 us: padded(): lax.ppermute(tail, axis, [(i, (i + 1) % count) for i in range(ends)])]
    ppermute x2 -> x0, local copies, waits for them, and re-layouts: 4.69 us -> none  [the longest x1 2.36 us: padded(): lax.ppermute(head, axis, [((i + 1) % count, i) for i in range(ends)])]
    unnamed x1 -> x0, blocking collectives: 4.29 us -> none
  transfers between devices with their start and end apart: 3 -> 0, of which waited for: 1 -> 0; matrix products, arithmetic and copies ran while one was open for 15% -> 0% of each run, Pallas kernels for 0% -> 0%
where the time goes in v3:
time: 14.5 us; the launch traced here: 14.3 us
  Pallas kernels  13 us (90%)
  between operations  0.66 us (5%)
  local copies, waits for them, and re-layouts  0.65 us (4%)
    pallas_call x1, Pallas kernels, per_device(): pl.pallas_call(functools.partial(stack_kernel, cfg), out_shape=pltpu.VMEM...  13 us
    unnamed x1, local copies, waits for them, and re-layouts  0.65 us

profile of v3, /device:TPU:0, one launch (start us, length us, event | category | flops | bytes accessed | tf_op | source)
XLA Modules:
  0.0 14.3 jit_solution(12715317186434234357)
XLA Ops:
  0.7 13.0 %shard_map.46 = f32[15,2,8,32]{3,2,1,0:T(8,128)S(1)} custom-call(bf16[4,2,64,256]{3,2,1,0:T(8,128)(2,1)} %scenes.1, s32[2,24]{1,0:T(2,128)} %bitcast.3, s32[1,1]{1,0:T(1,128)} %bitcast.2.count, f32[15,96]{1,0:T(8,128)} %inverse.1), custom_call_target="tpu_custom_call" | custom-call | tf_op jit(solution)/shard_map/pallas_call | solution.py:425
  13.7 0.7 %copy.6 = f32[15,2,8,32]{3,2,1,0:T(8,128)} copy(f32[15,2,8,32]{3,2,1,0:T(8,128)S(1)} %shard_map.46) | data formatting | bytes 61440

commit v4 on v3

--- a/solution.py
+++ b/solution.py
@@ -38,7 +38,7 @@
     local, base, dates_in, counts_in, edge_out, edge_in,
     raw, cells, total, h_high, h_low, weights, k_high, k_low, l_high, l_low,
     load_sem, send_sem, recv_sem, dates_send, dates_recv, count_send, count_recv, edge_send, edge_recv,
-    inverse_in, own_sem, edge_near, near_send, near_recv,
+    inverse_in, own_sem, looked,
 ):
     D, C, A, R, X, S, NP = (cfg[k] for k in ("D", "C", "A", "R", "X", "S", "NP"))
     T = X // 128
@@ -56,11 +56,13 @@
 
     @pl.when(has_left)
     def _():
-        pl.semaphore_signal(barrier, inc=1, device_id={"col": col - 1}, device_id_type=MESH)
+        for r in range(D):
+            pl.semaphore_signal(barrier, inc=1, device_id={"date": flipped(date, r), "col": col - 1}, device_id_type=MESH)
 
     @pl.when(has_right)
     def _():
-        pl.semaphore_signal(barrier, inc=1, device_id={"col": col + 1}, device_id_type=MESH)
+        for r in range(D):
+            pl.semaphore_signal(barrier, inc=1, device_id={"date": flipped(date, r), "col": col + 1}, device_id_type=MESH)
 
     load = pltpu.make_async_copy(scenes, local, load_sem)
     load.start()
@@ -87,13 +89,15 @@
     edge_out[0] = to_right.astype(BF16)
     edge_out[1] = to_left.astype(BF16)
 
-    for side, present in ((0, has_left), (1, has_right)):
-        @pl.when(jnp.logical_not(present))
-        def _():
-            edge_in[side] = jnp.zeros((D, R, 128), BF16)
-            edge_near[side] = jnp.zeros((D * R, 128), BF16)
-
-    pl.semaphore_wait(barrier, D - 1 + (has_left.astype(jnp.int32) + has_right.astype(jnp.int32)))
+    @pl.when(jnp.logical_not(has_left))
+    def _():
+        edge_in[0] = jnp.zeros((D, R, 128), BF16)
+
+    @pl.when(jnp.logical_not(has_right))
+    def _():
+        edge_in[1] = jnp.zeros((D, R, 128), BF16)
+
+    pl.semaphore_wait(barrier, D - 1 + D * (has_left.astype(jnp.int32) + has_right.astype(jnp.int32)))
 
     def rows_of(place):
         return pl.ds(pl.multiple_of(place * R, R), R)
@@ -111,30 +115,25 @@
             to_next["scene", r, begin] = remote(
                 scenes.at[begin:end, :, rows_of(there), :], base.at[r, begin:end],
                 send_sem.at[r, begin], recv_sem.at[r, begin], {"date": there})
-    near = (
-        remote(edge_out.at[0], edge_near.at[0], near_send.at[0], near_recv.at[0], {"col": col + 1}),
-        remote(edge_out.at[1], edge_near.at[1], near_send.at[1], near_recv.at[1], {"col": col - 1}),
-    )
-    for r in range(1, D):
+    for r in range(D):
         there = flipped(date, r)
-        for side in range(2):
-            to_next["edge", side, r] = remote(edge_near.at[side, rows_of(there)], edge_in.at[side, r], edge_send.at[side, r], edge_recv.at[side, r], {"date": there})
-
-    @pl.when(has_right)
-    def _():
-        near[0].start()
-
-    @pl.when(has_left)
-    def _():
-        near[1].start()
-
-    order_in = cfg["order_in"]
-    early = [r for r in order_in if r <= D // 2]
-    late = [r for r in order_in if r > D // 2]
-    for r in order_in[::-1]:
+        to_next["right", r] = remote(edge_out.at[0, rows_of(there)], edge_in.at[0, r], edge_send.at[0, r], edge_recv.at[0, r], {"date": there, "col": col + 1})
+        to_next["left", r] = remote(edge_out.at[1, rows_of(there)], edge_in.at[1, r], edge_send.at[1, r], edge_recv.at[1, r], {"date": there, "col": col - 1})
+    for r in order:
         to_next["dates", r].start()
         to_next["count", r].start()
-    for r in early:
+
+    @pl.when(has_right)
+    def _():
+        for r in order + [0]:
+            to_next["right", r].start()
+
+    @pl.when(has_left)
+    def _():
+        for r in order + [0]:
+            to_next["left", r].start()
+
+    for r in cfg["order_in"]:
         for begin, _ in cfg["cuts"][r]:
             to_next["scene", r, begin].start()
 
@@ -150,17 +149,6 @@
         value = jnp.where(inside, (8.0 - jnp.abs(offset.astype(F32) - 7.5)) / 128.0, 0.0)
         weights[c * TT * 128:(c + 1) * TT * 128, :] = value.astype(BF16)
 
-    for side, present in ((0, has_left), (1, has_right)):
-        @pl.when(present)
-        def _():
-            near[side].wait_recv()
-            for r in order_in[::-1]:
-                to_next["edge", side, r].start()
-
-    for r in late:
-        for begin, _ in cfg["cuts"][r]:
-            to_next["scene", r, begin].start()
-
     def unpack(slot, begin, end, main):
         many = end - begin
         for c in range(2):
@@ -168,8 +156,7 @@
                 for i in range(many):
                     at = ((c * TT + t) * many + i) * R
                     raw[at:at + R, :] = main(begin + i, c)[:, t * 128:(t + 1) * 128].astype(F32)
-        at_edge = [edge_in[n, slot] if slot else edge_near[n, rows_of(date), :] for n in range(2)]
-        edges = at_edge[0].astype(F32) + at_edge[1].astype(F32)
+        edges = edge_in[0, slot].astype(F32) + edge_in[1, slot].astype(F32)
         for c in range(2):
             for i in range(many):
                 at = ((c * TT + T) * many + i) * R
@@ -181,10 +168,13 @@
             cells[parity, :, slot * A + begin:slot * A + end] = got.reshape(2 * TT, many, half, 128)
 
     def wait_edges(r):
-        for side, present in ((0, has_left), (1, has_right)):
-            @pl.when(present)
-            def _():
-                to_next["edge", side, r].wait_recv()
+        @pl.when(has_left)
+        def _():
+            to_next["right", r].wait_recv()
+
+        @pl.when(has_right)
+        def _():
+            to_next["left", r].wait_recv()
 
     def product(p_at, s_at, t):
         real = imaginary = None
@@ -202,30 +192,30 @@
     def multiply(stage):
         at = stage["at"]
         rows = stage["rows"]
-        for t in range(TT):
-            for c in range(2):
-                where = (c * TT + t) * 128
-                parts = []
-                for r, j, q, n, _ in stage["pieces"]:
-                    if c == 0:
-                        made[r, j, q, t] = product(r * A + j, slice(q * A, q * A + n), t)
-                    parts.append(made[r, j, q, t][c].reshape(n * half, 128))
-                if rows > stage["used"]:
-                    parts.append(jnp.zeros((rows - stage["used"], 128), F32))
-                high, low = split(jnp.concatenate(parts, axis=0))
-                h_high[at:at + rows, where:where + 128] = high
-                h_low[at:at + rows, where:where + 128] = low
+        whole = [[p] for p in stage["pieces"] if p[2] != p[0]]
+        rest = [p for p in stage["pieces"] if p[2] == p[0]]
+        for group in whole + ([rest] if rest else []):
+            begin = at + group[0][4]
+            for t in range(TT):
+                parts = [product(r * A + j, slice(q * A, q * A + n), t) for r, j, q, n, _ in group]
+                for c in range(2):
+                    flat = [v[c].reshape(p[3] * half, 128) for v, p in zip(parts, group)]
+                    end = begin + sum(p[3] for p in group) * half
+                    if group is rest and end < at + rows:
+                        flat.append(jnp.zeros((at + rows - end, 128), F32))
+                        end = at + rows
+                    where = (c * TT + t) * 128
+                    high, low = split(flat[0] if len(flat) == 1 else jnp.concatenate(flat, axis=0))
+                    h_high[begin:end, where:where + 128] = high
+                    h_low[begin:end, where:where + 128] = low
         got = jnp.dot(h_high[at:at + rows, :], weights[...], preferred_element_type=F32)
         got = got + jnp.dot(h_low[at:at + rows, :], weights[...], preferred_element_type=F32)
-        signed = []
         for r, j, q, n, start in stage["pieces"]:
             sign = (2 * swapped(date, q, r) - 1).astype(F32) if q != r else -1.0
-            signed.append(got[start:start + n * half] * jnp.where(lanes < 64, 1.0, sign))
+            looked[start:start + n * half, :] = got[start:start + n * half] * jnp.where(lanes < 64, 1.0, sign)
         if rows > stage["used"]:
-            signed.append(got[stage["used"]:rows])
-        l_high[at:at + rows, :], l_low[at:at + rows, :] = split(jnp.concatenate(signed, axis=0))
-
-    made = {}
+            looked[stage["used"]:rows, :] = got[stage["used"]:rows]
+        l_high[at:at + rows, :], l_low[at:at + rows, :] = split(looked[0:rows, :])
 
     def invert(start, stop):
         rows = slice(start, stop)
@@ -242,6 +232,7 @@
             l_high[gap, :] = jnp.zeros((stage["padded"] - stage["rows"], 128), BF16)
             l_low[gap, :] = jnp.zeros((stage["padded"] - stage["rows"], 128), BF16)
 
+    wait_edges(0)
     unpack(0, 0, A, lambda i, c: local[i, c, rows_of(date), :])
     for copy in own:
         copy.wait()
@@ -269,15 +260,15 @@
         if key[0] in ("dates", "count", "scene"):
             copy.wait_send()
 
-    for side, come, go in ((0, has_left, has_right), (1, has_right, has_left)):
-        @pl.when(go)
-        def _():
-            near[side].wait_send()
-
-        @pl.when(come)
-        def _():
-            for r in range(1, D):
-                to_next["edge", side, r].wait_send()
+    @pl.when(has_right)
+    def _():
+        for r in range(D):
+            to_next["right", r].wait_send()
+
+    @pl.when(has_left)
+    def _():
+        for r in range(D):
+            to_next["left", r].wait_send()
 
 
 def swapped(date, low, high):
@@ -297,12 +288,11 @@
             if r == 1 and begin == 0:
                 news = [(0, j) for j in range(A)] + news
             pieces, used = [], 0
-            for slot, j in news:
-                for q in range(slot + 1):
-                    n = A if q < slot else j
-                    if n:
-                        pieces.append((slot, j, q, n, used))
-                        used += n * half
+            found = [(slot, j, q, A) for slot, j in news for q in range(slot)]
+            found += [(slot, j, slot, j) for slot, j in news if j]
+            for slot, j, q, n in found:
+                pieces.append((slot, j, q, n, used))
+                used += n * half
             rows = -(-used // 16) * 16
             padded = -(-used // 128) * 128
             stages.append(dict(arrive=[(r, begin, end)], pieces=pieces, used=used, rows=rows, padded=padded, at=at))
@@ -445,7 +435,8 @@
             pltpu.VMEM((total, 128), BF16),
             pltpu.VMEM((total, 128), BF16),
             dma, dma((D, A)), dma((D, A)), dma((D,)), dma((D,)), dma((D,)), dma((D,)), dma((2, D)), dma((2, D)),
-            pltpu.VMEM(inverse.shape, F32), dma((3,)), pltpu.VMEM((2, rows, 128), BF16), dma((2,)), dma((2,)),
+            pltpu.VMEM(inverse.shape, F32), dma((3,)),
+            pltpu.VMEM((max(stage["padded"] for stage in stages), 128), F32),
         ],
         compiler_params=pltpu.CompilerParams(collective_id=0, has_side_effects=True),
     )(scenes, pair_dates.T, pair_count.reshape(1, 1), inverse)

time: 14.5 us -> 13.7 us (0.945)
  Pallas kernels: 13 us -> 12.2 us
    pallas_call x1, Pallas kernels: 13 us -> 12.2 us  [per_device(): pl.pallas_call(functools.partial(stack_kernel, cfg), out_shape=pltpu.VMEM...]
where the time goes in v4:
time: 13.7 us; the launch traced here: 13.5 us
  Pallas kernels  12.2 us (89%)
  between operations  0.66 us (5%)
  local copies, waits for them, and re-layouts  0.65 us (5%)
    pallas_call x1, Pallas kernels, per_device(): pl.pallas_call(functools.partial(stack_kernel, cfg), out_shape=pltpu.VMEM...  12.2 us
    unnamed x1, local copies, waits for them, and re-layouts  0.65 us

profile of v4, /device:TPU:0, one launch (start us, length us, event | category | flops | bytes accessed | tf_op | source)
XLA Modules:
  0.0 13.5 jit_solution(7706238672712095919)
XLA Ops:
  0.7 12.2 %shard_map.46 = f32[15,2,8,32]{3,2,1,0:T(8,128)S(1)} custom-call(bf16[4,2,64,256]{3,2,1,0:T(8,128)(2,1)} %scenes.1, s32[2,24]{1,0:T(2,128)} %bitcast.3, s32[1,1]{1,0:T(1,128)} %bitcast.2.count, f32[15,96]{1,0:T(8,128)} %inverse.1), custom_call_target="tpu_custom_call" | custom-call | tf_op jit(solution)/shard_map/pallas_call | solution.py:415
  12.9 0.7 %copy.6 = f32[15,2,8,32]{3,2,1,0:T(8,128)} copy(f32[15,2,8,32]{3,2,1,0:T(8,128)S(1)} %shard_map.46) | data formatting | bytes 61440

commit v5 on v2

--- a/solution.py
+++ b/solution.py
@@ -38,7 +38,7 @@
     local, base, dates_in, counts_in, edge_out, edge_in,
     raw, cells, h_high, h_low, weights, k_high, k_low, l_high, l_low,
     load_sem, send_sem, recv_sem, dates_send, dates_recv, count_send, count_recv, edge_send, edge_recv,
-    inverse_in, own_sem,
+    inverse_in, own_sem, early,
 ):
     D, C, A, R, X, S, NP = (cfg[k] for k in ("D", "C", "A", "R", "X", "S", "NP"))
     dates_total = D * A
@@ -244,8 +244,17 @@
     wait_edges(0)
     unpack(0, lambda i, c: local[i, c, rows_of(date), :])
 
+    def invert(start, stop):
+        rows = slice(start * block, stop * block)
+        lh, ll = l_high[rows, :], l_low[rows, :]
+        kh = k_high[:, rows]
+        part = jnp.dot(kh, lh, preferred_element_type=F32)
+        part = part + jnp.dot(kh, ll, preferred_element_type=F32)
+        return part + jnp.dot(k_low[:, rows], lh, preferred_element_type=F32)
+
     order_in = cfg["order_in"]
     looked = 0
+    split_at = 0
     arrived = [0]
     for r in order_in:
         if r == order_in[0]:
@@ -254,6 +263,9 @@
             for q in range(1, D):
                 to_next["dates", q].wait_recv()
                 to_next["count", q].wait_recv()
+        if r == order_in[-1]:
+            split_at = looked
+            early[...] = invert(0, looked) if looked else jnp.zeros(early.shape, F32)
         wait_edges(r)
         to_next["scene", r].wait_recv()
         unpack(r, lambda i, c: base[r, i, c])
@@ -267,11 +279,7 @@
         if r == order_in[0]:
             invert_matrix(cfg, date, dates_in, counts_in, inverse_in, k_high, k_low, pair_order)
 
-    lh, ll = l_high[...], l_low[...]
-    kh = k_high[...]
-    series = jnp.dot(kh, lh, preferred_element_type=F32)
-    series = series + jnp.dot(kh, ll, preferred_element_type=F32)
-    series = series + jnp.dot(k_low[...], lh, preferred_element_type=F32)
+    series = early[...] + invert(split_at, len(chunks))
     for c in range(2):
         out[:, c] = series[:, c * 64:c * 64 + looks].reshape(NP, half, looks)
 
@@ -449,7 +457,7 @@
             pltpu.VMEM((total, 128), BF16),
             pltpu.VMEM((total, 128), BF16),
             dma, dma((D,)), dma((D,)), dma((D,)), dma((D,)), dma((D,)), dma((D,)), dma((2, D)), dma((2, D)),
-            pltpu.VMEM(inverse.shape, F32), dma((3,)),
+            pltpu.VMEM(inverse.shape, F32), dma((3,)), pltpu.VMEM((NP * half, 128), F32),
         ],
         compiler_params=pltpu.CompilerParams(collective_id=0, has_side_effects=True),
     )(scenes, pair_dates.T, pair_count.reshape(1, 1), inverse)

time: 12.8 us -> 12.9 us (level)
  no operation moved by 1% of the time
where the time goes in v5:
time: 12.9 us; the launch traced here: 12.7 us
  Pallas kernels  11.4 us (88%)
  between operations  0.66 us (5%)
  local copies, waits for them, and re-layouts  0.65 us (5%)
    pallas_call x1, Pallas kernels, per_device(): pl.pallas_call(functools.partial(stack_kernel, cfg), out_shape=pltpu.VMEM...  11.4 us
    unnamed x1, local copies, waits for them, and re-layouts  0.65 us

profile of v5, /device:TPU:0, one launch (start us, length us, event | category | flops | bytes accessed | tf_op | source)
XLA Modules:
  0.0 12.7 jit_solution(5292560349569599695)
XLA Ops:
  0.7 11.4 %shard_map.46 = f32[15,2,8,32]{3,2,1,0:T(8,128)S(1)} custom-call(bf16[4,2,64,256]{3,2,1,0:T(8,128)(2,1)} %scenes.1, s32[2,24]{1,0:T(2,128)} %bitcast.3, s32[1,1]{1,0:T(1,128)} %bitcast.2.count, f32[15,96]{1,0:T(8,128)} %inverse.1), custom_call_target="tpu_custom_call" | custom-call | tf_op jit(solution)/shard_map/pallas_call | solution.py:438
  12.1 0.7 %copy.6 = f32[15,2,8,32]{3,2,1,0:T(8,128)} copy(f32[15,2,8,32]{3,2,1,0:T(8,128)S(1)} %shard_map.46) | data formatting | bytes 61440
